TPU v7x, 256 devices: a whole 4x4x8 slice. The times are simulated.
256 devices in a mesh: ctx: 32 (over x, z), tp: 8 (over y, core).
Axes of the slice: x: 4, y: 4, z: 8, core: 2. Of those that a mesh axis runs over, the one named last changes fastest.
Arguments:
- tokens: bfloat16 [16384, 4096], P('ctx', 'tp'), may hold values from -16 to 16
- query_weight: bfloat16 [4096, 4096], P(None, 'tp'), may hold values from -0.09375 to 0.09375
- key_weight: bfloat16 [4096, 1024], P(None, 'tp'), may hold values from -0.09375 to 0.09375
- value_weight: bfloat16 [4096, 1024], P(None, 'tp'), may hold values from -0.09375 to 0.09375
- out_weight: bfloat16 [4096, 4096], P('tp'), may hold values from -0.09375 to 0.09375
- links: int32 [128, 16], P('ctx'), may hold values from 0 to 127, as said below
- counts: int32 [128], P('ctx'), may hold values from 1 to 16, as said below
- doc_ids: int32 [128], replicated, may hold values from 0 to 31, never falling along the last dimension, each value on 1 to 8 neighbouring positions
Outputs:
- mixed: bfloat16 [16384, 4096], P(('ctx', 'tp'))
Inputs may be any that keep to these rules, and one draw needn't show every extreme that they name: `links`: the first entry of each row is the query block itself; the entries of a row are distinct; every listed block lies within 4 ctx indices of its query block (block index // 4), and some query block of every ctx index lists a block exactly 4 indices away. `counts`: the first query block of each ctx index has 2 or more live slots, and block 0 has 16.
All inputs are finite; a program needn't handle non-finite values.
Results may differ from a plain program's by a relative error of at most 0.017.
Values may be sent and summed in bfloat16 or wider, within the bound.
No kernel may reach another device: no remote copies, remote signals or barrier semaphores. Data moves between devices by JAX's collectives and lax.ppermute only.
A program may use at most 64 MiB of HBM per device.

v0:
```python
import jax
import jax.numpy as jnp
from jax import lax
from jax.sharding import PartitionSpec as P

HEAD_DIM = 128
BLOCK = 128
LINKS = 16
REACH = 4


def from_behind(block, axis, distance):
    devices = range(lax.axis_size(axis))
    route = [(i - distance, i) for i in devices if i - distance in devices]
    return lax.ppermute(block, axis, route)


def local(tokens, query_weight, key_weight, value_weight, out_weight, links, counts, doc_ids):
    row_count = tokens.shape[0]
    query_width = query_weight.shape[1]
    key_width = key_weight.shape[1]
    piece = lax.all_gather(tokens, "tp", axis=1, tiled=True)
    weights = (query_weight, key_weight, value_weight)
    query, keys, values = tuple(
        (jnp.dot(piece, weight, preferred_element_type=jnp.float32) for weight in weights)
    )
    query = query.astype(jnp.bfloat16)
    block_count = row_count // BLOCK
    stacked = (
        jnp.stack([keys, values]).astype(jnp.bfloat16).reshape(2, block_count, BLOCK, key_width)
    )
    position = lax.axis_index("ctx")
    first_block = position * block_count
    pieces = []
    for offset in range(-REACH, REACH + 1):
        if offset == 0:
            pieces.append(stacked)
        else:
            pieces.append(from_behind(stacked, "ctx", -offset))
    source = jnp.concatenate(pieces, axis=1)
    anchor = (position - REACH) * block_count
    chosen = jnp.take(source, links - anchor, axis=1, mode="clip")
    kv_local = key_width // HEAD_DIM
    group = query_width // key_width
    chosen_keys = chosen[0].reshape(block_count, LINKS, BLOCK, kv_local, HEAD_DIM)
    chosen_values = chosen[1].reshape(block_count, LINKS, BLOCK, kv_local, HEAD_DIM)
    query_blocks = query.reshape(block_count, BLOCK, kv_local, group, HEAD_DIM)
    block_total = doc_ids.shape[0]
    table = jnp.arange(block_total, dtype=jnp.int32)
    query_index = first_block + jnp.arange(block_count, dtype=jnp.int32)[:, None]
    doc_key = jnp.sum(jnp.where(links[:, :, None] == table, doc_ids, 0), axis=-1)
    doc_query = jnp.sum(jnp.where(query_index == table[None, :], doc_ids[None, :], 0), axis=-1)[
        :, None
    ]
    live = jnp.arange(LINKS, dtype=jnp.int32)[None, :] < counts[:, None]
    earlier = (links < query_index) | (doc_key != doc_query)
    same = links == query_index
    causal = jnp.arange(BLOCK)[None, :] <= jnp.arange(BLOCK)[:, None]
    allowed = live[:, None, :, None] & (
        earlier[:, None, :, None] | same[:, None, :, None] & causal[None, :, None, :]
    )
    allowed = allowed[:, None, None]
    scores = jnp.einsum(
        "bqhgd,bskhd->bhgqsk", query_blocks, chosen_keys, preferred_element_type=jnp.float32
    ) * HEAD_DIM ** (-0.5)
    scores = jnp.where(allowed, scores, -1e30)
    top = jnp.max(scores, axis=(4, 5), keepdims=True)
    powers = jnp.where(allowed, jnp.exp(scores - top), 0.0)
    total = jnp.sum(powers, axis=(4, 5), keepdims=True)
    weights = (powers / total).astype(jnp.bfloat16)
    attended = jnp.einsum(
        "bhgqsk,bskhd->bqhgd", weights, chosen_values, preferred_element_type=jnp.float32
    )
    attended = attended.astype(jnp.bfloat16).reshape(row_count, query_width)
    return lax.psum_scatter(
        jnp.dot(attended, out_weight, preferred_element_type=jnp.float32).astype(jnp.bfloat16),
        "tp",
        scatter_dimension=0,
        tiled=True,
    )


def solution(mesh):
    placed = (
        P("ctx", "tp"),
        P(None, "tp"),
        P(None, "tp"),
        P(None, "tp"),
        P("tp", None),
        P("ctx", None),
        P("ctx"),
        P(),
    )
    return jax.shard_map(
        local, mesh=mesh, in_specs=placed, out_specs=P(("ctx", "tp"), None), check_vma=False
    )
```

profile of v0, /device:TPU:6, one launch (start us, length us, event | category | flops | bytes accessed | tf_op | source)
XLA Modules:
  0.0 212.3 jit_solution(15246871406914219502)
XLA Ops:
  6.5 0.7 all-gather.2.cloned.1.call-update
  7.3 0.0 reduce-scatter.2.cloned.1.call-start
  7.3 0.7 broadcast_subtract_fusion
  8.0 0.1 reshape.95
  8.1 0.8 select_reduce_fusion.1
  9.0 0.9 select_reduce_fusion
  9.9 0.7 iota_compare_fusion.3
  10.6 0.8 compare_or_fusion
  11.4 3.7 %or_and_fusion = pred[4,128,16,128]{1,3,2,0:T(8,128)(4,1)} fusion(pred[128,128]{0,1:T(8,128)(4,1)S(1)} %iota_compare_fusion, pred[4,16]{1,0:T(4,128)(4,1)S(1)} %get-tuple-element.6, pred[4,16]{1,0:T(4,128)(4,1)S(1)} %get-tuple-element.5, pred[4,16]{1,0:T(4,128)(4,1)S(1)} %iota_compare_fusion.3), kind=kLoop, calls=%fused_computation.9 | loop fusion | flops 3145728 | bytes 1065152 | tf_op jit(solution)/shard_map/and | solution.py:59
  15.0 31.7 %all-gather.2.cloned.1.call-done = bf16[512,4096]{1,0:T(8,128)(2,1)} async-done(((bf16[512,512]{1,0:T(8,128)(2,1)}), bf16[512,4096]{1,0:T(8,128)(2,1)}) %all-gather.2.cloned.1.call-update) | async-done | bytes 4194320 | tf_op jit(solution)/shard_map/all_gather | solution.py:22
  46.7 3.6 %convolution_convert_fusion.2 = bf16[512,128]{1,0:T(8,128)(2,1)S(1)} fusion(bf16[512,4096]{1,0:T(8,128)(2,1)} %all-gather.2.cloned.1.call-done, bf16[4096,128]{1,0:T(8,128)(2,1)S(1)} %copy-done), kind=kOutput, calls=%fused_computation.17 | convolution fusion | flops 536936448 | bytes 5373952 | tf_op jit(solution)/shard_map/dot_general | solution.py:25
  50.3 0.0 copy-start.6
  50.4 1.3 convolution_convert_fusion.3
  51.6 0.7 pad_maximum_fusion
  52.4 7.9 %collective-permute-start.7 = (bf16[2,4,128,128]{3,2,1,0:T(8,128)(2,1)}, bf16[2,4,128,128]{3,2,1,0:T(8,128)(2,1)}, u32[]{:S(2)}, u32[]{:S(2)}) collective-permute-start(bf16[2,4,128,128]{3,2,1,0:T(8,128)(2,1)} %pad_maximum_fusion), channel_id=1, source_target_pairs={{32,0},{40,8},{48,16},{56,24},{64,32},{72,40},{80,48},{88,56},{96,... | collective-permute-start | bytes 786440 | tf_op jit(solution)/shard_map/ppermute | solution.py:15
  60.3 2.2 %collective-permute-start.6 = (bf16[2,4,128,128]{3,2,1,0:T(8,128)(2,1)}, bf16[2,4,128,128]{3,2,1,0:T(8,128)(2,1)}, u32[]{:S(2)}, u32[]{:S(2)}) collective-permute-start(bf16[2,4,128,128]{3,2,1,0:T(8,128)(2,1)} %pad_maximum_fusion), channel_id=1, source_target_pairs={{24,0},{32,8},{40,16},{48,24},{56,32},{64,40},{72,48},{80,56},{88,... | collective-permute-start | bytes 786440 | tf_op jit(solution)/shard_map/ppermute | solution.py:15
  62.5 4.5 %collective-permute-start.2 = (bf16[2,4,128,128]{3,2,1,0:T(8,128)(2,1)}, bf16[2,4,128,128]{3,2,1,0:T(8,128)(2,1)}, u32[]{:S(2)}, u32[]{:S(2)}) collective-permute-start(bf16[2,4,128,128]{3,2,1,0:T(8,128)(2,1)} %pad_maximum_fusion), channel_id=1, source_target_pairs={{0,16},{8,24},{16,32},{24,40},{32,48},{40,56},{48,64},{56,72},{64,... | collective-permute-start | bytes 786440 | tf_op jit(solution)/shard_map/ppermute | solution.py:15
  67.0 5.5 %collective-permute-start.1 = (bf16[2,4,128,128]{3,2,1,0:T(8,128)(2,1)}, bf16[2,4,128,128]{3,2,1,0:T(8,128)(2,1)}, u32[]{:S(2)}, u32[]{:S(2)}) collective-permute-start(bf16[2,4,128,128]{3,2,1,0:T(8,128)(2,1)} %pad_maximum_fusion), channel_id=1, source_target_pairs={{0,24},{8,32},{16,40},{24,48},{32,56},{40,64},{48,72},{56,80},{64,... | collective-permute-start | bytes 786440 | tf_op jit(solution)/shard_map/ppermute | solution.py:15
  72.5 2.0 collective-permute-start
  74.6 2.3 %convolution_convert_fusion.1 = bf16[512,512]{1,0:T(8,128)(2,1)S(1)} fusion(bf16[512,4096]{1,0:T(8,128)(2,1)S(1)} %copy-done.7, bf16[4096,512]{1,0:T(8,128)(2,1)S(1)} %copy-done.6), kind=kOutput, calls=%fused_computation.14 | convolution fusion | flops 2147745792 | bytes 8912896 | tf_op jit(solution)/shard_map/dot_general | solution.py:25
  76.9 0.9 reshape.90
  77.8 32.8 %collective-permute-done = bf16[2,4,128,128]{3,2,1,0:T(8,128)(2,1)S(1)} collective-permute-done((bf16[2,4,128,128]{3,2,1,0:T(8,128)(2,1)}, bf16[2,4,128,128]{3,2,1,0:T(8,128)(2,1)S(1)}, u32[]{:S(2)}, u32[]{:S(2)}) %collective-permute-start) | collective-permute-done | bytes 262176 | tf_op jit(solution)/shard_map/ppermute | solution.py:15
  110.6 0.7 copy-done.5
  111.4 1.9 collective-permute-start.3
  113.3 1.0 constant_dynamic-update-slice_fusion.8
  114.2 0.0 collective-permute-done.1
  114.2 7.4 %collective-permute-start.5 = (bf16[2,4,128,128]{3,2,1,0:T(8,128)(2,1)}, bf16[2,4,128,128]{3,2,1,0:T(8,128)(2,1)S(1)}, u32[]{:S(2)}, u32[]{:S(2)}) collective-permute-start(bf16[2,4,128,128]{3,2,1,0:T(8,128)(2,1)} %pad_maximum_fusion), channel_id=1, source_target_pairs={{16,0},{24,8},{32,16},{40,24},{48,32},{56,40},{64,48},{72,56},{80,... | collective-permute-start | bytes 786440 | tf_op jit(solution)/shard_map/ppermute | solution.py:15
  121.7 1.0 constant_dynamic-update-slice_fusion.7
  122.7 0.0 collective-permute-done.2
  122.7 4.1 %collective-permute-start.4 = (bf16[2,4,128,128]{3,2,1,0:T(8,128)(2,1)}, bf16[2,4,128,128]{3,2,1,0:T(8,128)(2,1)S(1)}, u32[]{:S(2)}, u32[]{:S(2)}) collective-permute-start(bf16[2,4,128,128]{3,2,1,0:T(8,128)(2,1)} %pad_maximum_fusion), channel_id=1, source_target_pairs={{8,0},{16,8},{24,16},{32,24},{40,32},{48,40},{56,48},{64,56},{72,6... | collective-permute-start | bytes 786440 | tf_op jit(solution)/shard_map/ppermute | solution.py:15
  126.8 1.0 constant_dynamic-update-slice_fusion.6
  127.8 0.0 collective-permute-done.3
  127.9 0.9 constant_dynamic-update-slice_fusion.4
  128.8 9.5 %collective-permute-done.4 = bf16[2,4,128,128]{3,2,1,0:T(8,128)(2,1)S(1)} collective-permute-done((bf16[2,4,128,128]{3,2,1,0:T(8,128)(2,1)}, bf16[2,4,128,128]{3,2,1,0:T(8,128)(2,1)S(1)}, u32[]{:S(2)}, u32[]{:S(2)}) %collective-permute-start.4) | collective-permute-done | bytes 262176 | tf_op jit(solution)/shard_map/ppermute | solution.py:15
  138.4 0.0 collective-permute-done.5
  138.4 0.0 collective-permute-done.6
  138.4 1.0 constant_dynamic-update-slice_fusion.1
  139.4 0.0 collective-permute-done.7
  139.4 1.0 constant_dynamic-update-slice_fusion
  140.4 3.0 %gather_fusion = bf16[64,2,128,128]{3,2,1,0:T(8,128)(2,1)} fusion(bf16[2,36,128,128]{3,2,1,0:T(8,128)(2,1)S(1)} %constant_dynamic-update-slice_fusion, s32[1024]{0:T(1024)S(1)} %pad_clamp_fusion), kind=kCustom, calls=%fused_computation | custom fusion | bytes 8388864 | tf_op jit(solution)/shard_map/jit(_take)/gather | solution.py:42
  143.5 2.9 %copy.18 = bf16[64,2,128,128]{3,2,0,1:T(8,128)(2,1)S(1)} copy(bf16[64,2,128,128]{3,2,1,0:T(8,128)(2,1)} %gather_fusion) | data formatting | bytes 8388608 | tf_op jit(solution)/shard_map/jit(_take)/gather | solution.py:42
  146.4 2.6 %fusion = (f32[4,4,128]{2,1,0:T(4,128)S(1)}, f32[4,16,128,128,4]{3,2,4,1,0:T(8,128)S(1)}) fusion(pred[4,128,16,128]{1,3,2,0:T(8,128)(4,1)S(1)} %copy-done.1, bf16[4,128,4,128,1]{3,2,1,0,4:T(4,128)(2,1)S(1)} %bitcast.87, bf16[2,4,16,128,128]{4,3,2,1,0:T(8,128)(2,1)S(1)} %bitcast.85), kind=kOutput, calls=%fused_computation.4 | convolution fusion | flops 1086322688 | bytes 20455424 | tf_op jit(solution)/shard_map/bqhgd,bskhd->bhgqsk/dot_general | solution.py:63
  149.0 4.3 %fusion.1 = f32[4,4,128]{2,1,0:T(4,128)S(1)} fusion(f32[4,16,128,128,4]{3,2,4,1,0:T(8,128)S(1)} %get-tuple-element.8, f32[4,4,128]{2,1,0:T(4,128)S(1)} %get-tuple-element.7, pred[4,128,16,128]{1,3,2,0:T(8,128)(4,1)S(1)} %copy-done.1), kind=kLoop, calls=%fused_computation.5 | loop fusion | flops 20969472 | bytes 17842176 | tf_op jit(solution)/shard_map/reduce_sum | solution.py:69
  153.2 6.3 %fusion.11 = bf16[4,128,1,4,128]{1,4,3,0,2:T(8,128)(2,1)S(1)} fusion(f32[4,4,128]{2,1,0:T(4,128)S(1)} %fusion.1, f32[4,4,128]{2,1,0:T(4,128)S(1)} %get-tuple-element.7, f32[4,16,128,128,4]{3,2,4,1,0:T(8,128)S(1)} %get-tuple-element.8, pred[4,128,16,128]{1,3,2,0:T(8,128)(4,1)S(1)} %copy-done.1, bf16[2,4,16,128,128]{4,3,2,1,0:T(8,128)(2,1)} %bitcast.86), kind=kOutput, calls=%fused_computation.16 | convolution fusion | flops 1099169792 | bytes 20463616 | tf_op jit(solution)/shard_map/bhgqsk,bskhd->bqhgd/dot_general | solution.py:71
  159.5 0.3 copy.22
  159.8 6.5 %convolution_convert_fusion = bf16[512,4096]{1,0:T(8,128)(2,1)} fusion(bf16[512,4096]{1,0:T(8,128)(2,1)} %param.12, bf16[64,8,4,128]{3,2,1,0:T(4,128)(2,1)S(1)} %bitcast.88), kind=kOutput, calls=%fused_computation.8 | convolution fusion | flops 2149580800 | bytes 8912896 | tf_op jit(solution)/shard_map/dot_general | solution.py:76
  166.3 0.0 reduce-scatter.2.cloned.1.call-update
  166.3 39.1 %reduce-scatter.2.cloned.1.call-done = bf16[64,4096]{1,0:T(8,128)(2,1)} async-done(((bf16[512,4096]{1,0:T(8,128)(2,1)}), bf16[64,4096]{1,0:T(8,128)(2,1)}) %reduce-scatter.2.cloned.1.call-update) | async-done | bytes 524304 | tf_op jit(solution)/shard_map/reduce_scatter | solution.py:75
  (23 shorter events, 0.2 us)
Async XLA Ops:
  6.5 40.2 %copy-start = (bf16[4096,128]{1,0:T(8,128)(2,1)S(1)}, bf16[4096,128]{1,0:T(8,128)(2,1)}, u32[]{:S(2)}) copy-start(bf16[4096,128]{1,0:T(8,128)(2,1)} %param.11) | copy-start | bytes 3145732
  6.5 43.8 %copy-start.8 = (bf16[4096,128]{1,0:T(8,128)(2,1)S(1)}, bf16[4096,128]{1,0:T(8,128)(2,1)}, u32[]{:S(2)}) copy-start(bf16[4096,128]{1,0:T(8,128)(2,1)} %param.10) | copy-start | bytes 3145732
  6.5 40.2 %all-gather.2.cloned.1.call-start = ((), (), s32[]{:S(2)}) async-start(), calls=%async_computation.1 | async-start | bytes 4718592 | tf_op jit(solution)/shard_map/all_gather | solution.py:22
  7.3 198.2 %reduce-scatter.2.cloned.1.call-start = ((), (), s32[]{:S(2)}) async-start(), calls=%async_computation.2 | async-start | bytes 4718592 | tf_op jit(solution)/shard_map/reduce_scatter | solution.py:75
  46.7 3.6 %copy-start.7 = (bf16[512,4096]{1,0:T(8,128)(2,1)S(1)}, bf16[512,4096]{1,0:T(8,128)(2,1)}, u32[]{:S(2)}) copy-start(bf16[512,4096]{1,0:T(8,128)(2,1)} %all-gather.2.cloned.1.call-done) | copy-start | bytes 12582916
  50.3 24.2 %copy-start.6 = (bf16[4096,512]{1,0:T(8,128)(2,1)S(1)}, bf16[4096,512]{1,0:T(8,128)(2,1)}, u32[]{:S(2)}) copy-start(bf16[4096,512]{1,0:T(8,128)(2,1)} %param.9) | copy-start | bytes 12582916
  51.6 20.9 %copy-start.4 = (bf16[512,128]{1,0:T(8,128)(2,1)}, bf16[512,128]{1,0:T(8,128)(2,1)S(1)}, u32[]{:S(2)}) copy-start(bf16[512,128]{1,0:T(8,128)(2,1)S(1)} %convolution_convert_fusion.3) | copy-start | bytes 393220
  52.4 87.0 %collective-permute-start.7 = (bf16[2,4,128,128]{3,2,1,0:T(8,128)(2,1)}, bf16[2,4,128,128]{3,2,1,0:T(8,128)(2,1)}, u32[]{:S(2)}, u32[]{:S(2)}) collective-permute-start(bf16[2,4,128,128]{3,2,1,0:T(8,128)(2,1)} %pad_maximum_fusion), channel_id=1, source_target_pairs={{32,0},{40,8},{48,16},{56,24},{64,32},{72,40},{80,48},{88,56},{96,... | collective-permute-start | bytes 786440 | tf_op jit(solution)/shard_map/ppermute | solution.py:15
  60.3 78.1 %collective-permute-start.6 = (bf16[2,4,128,128]{3,2,1,0:T(8,128)(2,1)}, bf16[2,4,128,128]{3,2,1,0:T(8,128)(2,1)}, u32[]{:S(2)}, u32[]{:S(2)}) collective-permute-start(bf16[2,4,128,128]{3,2,1,0:T(8,128)(2,1)} %pad_maximum_fusion), channel_id=1, source_target_pairs={{24,0},{32,8},{40,16},{48,24},{56,32},{64,40},{72,48},{80,56},{88,... | collective-permute-start | bytes 786440 | tf_op jit(solution)/shard_map/ppermute | solution.py:15
  62.5 60.2 %collective-permute-start.2 = (bf16[2,4,128,128]{3,2,1,0:T(8,128)(2,1)}, bf16[2,4,128,128]{3,2,1,0:T(8,128)(2,1)}, u32[]{:S(2)}, u32[]{:S(2)}) collective-permute-start(bf16[2,4,128,128]{3,2,1,0:T(8,128)(2,1)} %pad_maximum_fusion), channel_id=1, source_target_pairs={{0,16},{8,24},{16,32},{24,40},{32,48},{40,56},{48,64},{56,72},{64,... | collective-permute-start | bytes 786440 | tf_op jit(solution)/shard_map/ppermute | solution.py:15
  67.0 47.3 %collective-permute-start.1 = (bf16[2,4,128,128]{3,2,1,0:T(8,128)(2,1)}, bf16[2,4,128,128]{3,2,1,0:T(8,128)(2,1)}, u32[]{:S(2)}, u32[]{:S(2)}) collective-permute-start(bf16[2,4,128,128]{3,2,1,0:T(8,128)(2,1)} %pad_maximum_fusion), channel_id=1, source_target_pairs={{0,24},{8,32},{16,40},{24,48},{32,56},{40,64},{48,72},{56,80},{64,... | collective-permute-start | bytes 786440 | tf_op jit(solution)/shard_map/ppermute | solution.py:15
  72.5 38.1 %collective-permute-start = (bf16[2,4,128,128]{3,2,1,0:T(8,128)(2,1)}, bf16[2,4,128,128]{3,2,1,0:T(8,128)(2,1)S(1)}, u32[]{:S(2)}, u32[]{:S(2)}) collective-permute-start(bf16[2,4,128,128]{3,2,1,0:T(8,128)(2,1)} %pad_maximum_fusion), channel_id=1, source_target_pairs={{0,32},{8,40},{16,48},{24,56},{32,64},{40,72},{48,80},{56,88},{64,... | collective-permute-start | bytes 786440 | tf_op jit(solution)/shard_map/ppermute | solution.py:15
  110.6 0.7 copy-start.5
  111.4 16.5 %collective-permute-start.3 = (bf16[2,4,128,128]{3,2,1,0:T(8,128)(2,1)}, bf16[2,4,128,128]{3,2,1,0:T(8,128)(2,1)S(1)}, u32[]{:S(2)}, u32[]{:S(2)}) collective-permute-start(bf16[2,4,128,128]{3,2,1,0:T(8,128)(2,1)} %pad_maximum_fusion), channel_id=1, source_target_pairs={{0,8},{8,16},{16,24},{24,32},{32,40},{40,48},{48,56},{56,64},{64,7... | collective-permute-start | bytes 786440 | tf_op jit(solution)/shard_map/ppermute | solution.py:15
  114.2 24.1 %collective-permute-start.5 = (bf16[2,4,128,128]{3,2,1,0:T(8,128)(2,1)}, bf16[2,4,128,128]{3,2,1,0:T(8,128)(2,1)S(1)}, u32[]{:S(2)}, u32[]{:S(2)}) collective-permute-start(bf16[2,4,128,128]{3,2,1,0:T(8,128)(2,1)} %pad_maximum_fusion), channel_id=1, source_target_pairs={{16,0},{24,8},{32,16},{40,24},{48,32},{56,40},{64,48},{72,56},{80,... | collective-permute-start | bytes 786440 | tf_op jit(solution)/shard_map/ppermute | solution.py:15
  122.7 15.6 %collective-permute-start.4 = (bf16[2,4,128,128]{3,2,1,0:T(8,128)(2,1)}, bf16[2,4,128,128]{3,2,1,0:T(8,128)(2,1)S(1)}, u32[]{:S(2)}, u32[]{:S(2)}) collective-permute-start(bf16[2,4,128,128]{3,2,1,0:T(8,128)(2,1)} %pad_maximum_fusion), channel_id=1, source_target_pairs={{8,0},{16,8},{24,16},{32,24},{40,32},{48,40},{56,48},{64,56},{72,6... | collective-permute-start | bytes 786440 | tf_op jit(solution)/shard_map/ppermute | solution.py:15
  143.4 2.9 %copy-start.1 = (pred[4,128,16,128]{1,3,2,0:T(8,128)(4,1)S(1)}, pred[4,128,16,128]{1,3,2,0:T(8,128)(4,1)}, u32[]{:S(2)}) copy-start(pred[4,128,16,128]{1,3,2,0:T(8,128)(4,1)} %or_and_fusion) | copy-start | bytes 3145732
  143.5 2.9 %copy-start.3 = (bf16[4,128,4,128]{3,2,1,0:T(4,128)(2,1)S(1)}, bf16[4,128,4,128]{3,2,1,0:T(4,128)(2,1)}, u32[]{:S(2)}) copy-start(bf16[4,128,4,128]{3,2,1,0:T(4,128)(2,1)} %reshape.90) | copy-start | bytes 1572868
  146.3 2.6 %copy-start.2 = (bf16[64,2,128,128]{3,2,0,1:T(8,128)(2,1)}, bf16[64,2,128,128]{3,2,0,1:T(8,128)(2,1)S(1)}, u32[]{:S(2)}) copy-start(bf16[64,2,128,128]{3,2,0,1:T(8,128)(2,1)S(1)} %copy.18) | copy-start | bytes 12582916
Sparse Core Ops, SparseCore 0:
  9.2 37.5 all-gather.1
  166.5 38.9 reduce-scatter.1
where the time goes:
time: 213 us; the launch traced here: 212 us
  waiting for transfers between devices  114 us (54%)
  starting transfers between devices  35.6 us (17%)
  matrix products  22.5 us (11%)
  between operations  13.7 us (6%)
  other arithmetic  13.6 us (6%)
  local copies, waits for them, and re-layouts  13 us (6%)
    ppermute x8, waiting for transfers between devices, from_behind(): return lax.ppermute(block, axis, route)  42.4 us
    reduce_scatter x1, waiting for transfers between devices, local(): lax.psum_scatter(jnp.dot(attended, out_weight, preferred_element_type=jnp...  39.1 us
    ppermute x8, starting transfers between devices, from_behind(): return lax.ppermute(block, axis, route)  35.6 us
    all_gather x1, waiting for transfers between devices, local(): piece = lax.all_gather(tokens, 'tp', axis=1, tiled=True)  31.7 us
    dot_general x3, matrix products, local(): jnp.dot(piece, weight, preferred_element_type=jnp.float32)  7.17 us
    dot_general x1, matrix products, local(): jnp.dot(attended, out_weight, preferred_element_type=jnp.float32)  6.49 us
    dot_general x1, matrix products, local(): jnp.einsum('bhgqsk,bskhd->bqhgd', weights, chosen_values, preferred_eleme...  6.27 us
    gather x2, local copies, waits for them, and re-layouts, local(): chosen = jnp.take(source, links - anchor, axis=1, mode='clip')  5.91 us
  transfers between devices with their start and end apart: 10, of which 4 were waited for; matrix products, arithmetic and copies ran while one was open for 8% of the time, Pallas kernels for 0%

commit v1 on v0

--- a/solution.py
+++ b/solution.py
@@ -19,7 +19,9 @@
     row_count = tokens.shape[0]
     query_width = query_weight.shape[1]
     key_width = key_weight.shape[1]
-    piece = lax.all_gather(tokens, "tp", axis=1, tiled=True)
+    piece = jnp.concatenate(
+        lax.all_to_all(jnp.stack([tokens] * lax.axis_size("tp")), "tp", 0, 0), axis=1
+    )
     weights = (query_weight, key_weight, value_weight)
     query, keys, values = tuple(
         (jnp.dot(piece, weight, preferred_element_type=jnp.float32) for weight in weights)

time: 213 us -> 244 us (1.15)
  local copies, waits for them, and re-layouts: 13 us -> 36 us
  other arithmetic: 13.6 us -> 9.29 us
  waiting for transfers between devices: 114 us -> 118 us
  starting transfers between devices: 35.6 us -> 39.4 us
  matrix products: 22.5 us -> 26.1 us
    all_to_all x0 -> x1, waiting for transfers between devices: none -> 45.3 us  [local(): lax.all_to_all(jnp.stack([tokens] * lax.axis_size('tp')), 'tp', 0, 0)]
    all_gather x1 -> x0, waiting for transfers between devices: 31.7 us -> none  [local(): piece = lax.all_gather(tokens, 'tp', axis=1, tiled=True)]
    another operation x1 -> x3, local copies, waits for them, and re-layouts: 0.92 us -> 11.8 us
    all_to_all x0 -> x1, local copies, waits for them, and re-layouts: none -> 6.52 us  [local(): lax.all_to_all(jnp.stack([tokens] * lax.axis_size('tp')), 'tp', 0, 0)]
    reshape x0 -> x1, local copies, waits for them, and re-layouts: none -> 6.49 us  [local(): jnp.concatenate(lax.all_to_all(jnp.stack([tokens] * lax.axis_size('tp')),...]
    ppermute x8, waiting for transfers between devices: 42.4 us -> 36.8 us  [from_behind(): return lax.ppermute(block, axis, route)]
    all_to_all x0 -> x1, starting transfers between devices: none -> 4.67 us  [local(): lax.all_to_all(jnp.stack([tokens] * lax.axis_size('tp')), 'tp', 0, 0)]
    dot_general x3, matrix products: 7.17 us -> 10.6 us  [local(): jnp.dot(piece, weight, preferred_element_type=jnp.float32)]
  transfers between devices with their start and end apart: 10 -> 10, of which waited for: 4 -> 4; matrix products, arithmetic and copies ran while one was open for 8% -> 9% of each run, Pallas kernels for 0% -> 0%
where the time goes in v1:
time: 244 us; the launch traced here: 243 us
  waiting for transfers between devices  118 us (48%)
  starting transfers between devices  39.4 us (16%)
  local copies, waits for them, and re-layouts  36 us (15%)
  matrix products  26.1 us (11%)
  between operations  13.7 us (6%)
  other arithmetic  9.29 us (4%)
    all_to_all x1, waiting for transfers between devices, local(): lax.all_to_all(jnp.stack([tokens] * lax.axis_size('tp')), 'tp', 0, 0)  45.3 us
    ppermute x8, waiting for transfers between devices, from_behind(): return lax.ppermute(block, axis, route)  36.8 us
    reduce_scatter x1, waiting for transfers between devices, local(): lax.psum_scatter(jnp.dot(attended, out_weight, preferred_element_type=jnp...  36.3 us
    ppermute x8, starting transfers between devices, from_behind(): return lax.ppermute(block, axis, route)  34.7 us
    dot_general x3, matrix products, local(): jnp.dot(piece, weight, preferred_element_type=jnp.float32)  10.6 us
    another operation x2, local copies, waits for them, and re-layouts  8.31 us
    dot_general x1, matrix products, local(): jnp.dot(attended, out_weight, preferred_element_type=jnp.float32)  6.58 us
    all_to_all x1, local copies, waits for them, and re-layouts, local(): lax.all_to_all(jnp.stack([tokens] * lax.axis_size('tp')), 'tp', 0, 0)  6.52 us
  transfers between devices with their start and end apart: 10, of which 4 were waited for; matrix products, arithmetic and copies ran while one was open for 9% of the time, Pallas kernels for 0%

profile of v1, /device:TPU:6, one launch (start us, length us, event | category | flops | bytes accessed | tf_op | source)
XLA Modules:
  0.0 243.0 jit_solution(17653229663786581388)
XLA Ops:
  6.5 3.5 %stack.4 = bf16[8,512,512]{2,1,0:T(8,128)(2,1)} broadcast(bf16[512,512]{1,0:T(8,128)(2,1)} %param.8), dimensions={1,2} | broadcast | bytes 4718592 | tf_op jit(solution)/shard_map/stack | solution.py:23
  10.0 4.7 %all-to-all-start = ((bf16[8,512,512]{2,1,0:T(8,128)(2,1)}), bf16[8,512,512]{2,1,0:T(8,128)(2,1)}, u32[]{:S(2)}, u32[]{:S(2)}) async-start(bf16[8,512,512]{2,1,0:T(8,128)(2,1)} %stack.4), calls=%async_computation | async-start | bytes 8388608 | tf_op jit(solution)/shard_map/all_to_all | solution.py:23
  14.7 0.0 reduce-scatter.2.cloned.1.call-start
  14.8 0.1 reshape.118
  14.9 0.2 select_reduce_fusion.1
  15.1 0.2 select_reduce_fusion
  15.3 0.1 compare_or_fusion
  15.4 3.7 %or_and_fusion = pred[4,128,16,128]{1,3,2,0:T(8,128)(4,1)} fusion(pred[128,128]{0,1:T(8,128)(4,1)S(1)} %iota_compare_fusion, pred[4,16]{1,0:T(4,128)(4,1)S(1)} %get-tuple-element.6, pred[4,16]{1,0:T(4,128)(4,1)S(1)} %get-tuple-element.5, pred[4,16]{1,0:T(4,128)(4,1)S(1)} %get-tuple-element.9), kind=kLoop, calls=%fused_computation.10 | loop fusion | flops 3145728 | bytes 1065152 | tf_op jit(solution)/shard_map/and | solution.py:61
  19.1 45.3 %all-to-all-done = bf16[8,512,512]{2,1,0:T(8,128)(2,1)} async-done(((bf16[8,512,512]{2,1,0:T(8,128)(2,1)}), bf16[8,512,512]{2,1,0:T(8,128)(2,1)}, u32[]{:S(2)}, u32[]{:S(2)}) %all-to-all-start) | async-done | bytes 4194336 | tf_op jit(solution)/shard_map/all_to_all | solution.py:23
  64.3 6.5 %copy.32 = bf16[512,8,512]{2,1,0:T(8,128)(2,1)} copy(bf16[512,8,512]{2,0,1:T(8,128)(2,1)} %bitcast.1) | data formatting | bytes 8388608 | tf_op jit(solution)/shard_map/reshape | solution.py:22
  70.8 7.4 %reshape.109 = bf16[4,128,4096]{2,1,0:T(8,128)(2,1)} reshape(bf16[512,8,512]{2,1,0:T(8,128)(2,1)} %copy.32) | data formatting | bytes 8388608 | tf_op jit(solution)/shard_map/reshape.78
  78.2 3.6 %fusion.15 = bf16[1,4,128,128]{3,2,1,0:T(8,128)(2,1)S(1)} fusion(bf16[4,128,4096]{2,1,0:T(8,128)(2,1)} %reshape.109, bf16[4096,128]{1,0:T(8,128)(2,1)S(1)} %copy-done), kind=kOutput, calls=%fused_computation.21 | convolution fusion | flops 536936448 | bytes 5373952 | tf_op jit(solution)/shard_map/dot_general | solution.py:27
  81.8 0.1 copy-done.10
  82.0 1.2 fusion.14
  83.2 0.7 pad_maximum_fusion
  84.0 9.3 %collective-permute-start.7 = (bf16[2,4,128,128]{3,2,1,0:T(8,128)(2,1)}, bf16[2,4,128,128]{3,2,1,0:T(8,128)(2,1)S(1)}, u32[]{:S(2)}, u32[]{:S(2)}) collective-permute-start(bf16[2,4,128,128]{3,2,1,0:T(8,128)(2,1)} %pad_maximum_fusion), channel_id=1, source_target_pairs={{32,0},{40,8},{48,16},{56,24},{64,32},{72,40},{80,48},{88,56},{96,... | collective-permute-start | bytes 786440 | tf_op jit(solution)/shard_map/ppermute | solution.py:15
  93.3 1.9 collective-permute-start.6
  95.3 4.4 %collective-permute-start.2 = (bf16[2,4,128,128]{3,2,1,0:T(8,128)(2,1)}, bf16[2,4,128,128]{3,2,1,0:T(8,128)(2,1)}, u32[]{:S(2)}, u32[]{:S(2)}) collective-permute-start(bf16[2,4,128,128]{3,2,1,0:T(8,128)(2,1)} %pad_maximum_fusion), channel_id=1, source_target_pairs={{0,16},{8,24},{16,32},{24,40},{32,48},{40,56},{48,64},{56,72},{64,... | collective-permute-start | bytes 786440 | tf_op jit(solution)/shard_map/ppermute | solution.py:15
  99.6 6.7 %collective-permute-start.1 = (bf16[2,4,128,128]{3,2,1,0:T(8,128)(2,1)}, bf16[2,4,128,128]{3,2,1,0:T(8,128)(2,1)}, u32[]{:S(2)}, u32[]{:S(2)}) collective-permute-start(bf16[2,4,128,128]{3,2,1,0:T(8,128)(2,1)} %pad_maximum_fusion), channel_id=1, source_target_pairs={{0,24},{8,32},{16,40},{24,48},{32,56},{40,64},{48,72},{56,80},{64,... | collective-permute-start | bytes 786440 | tf_op jit(solution)/shard_map/ppermute | solution.py:15
  106.3 2.4 collective-permute-start
  108.7 6.5 %copy.31 = bf16[8,512,512]{1,2,0:T(8,128)(2,1)} copy(bf16[8,512,512]{2,1,0:T(8,128)(2,1)} %all-to-all-done) | data formatting | bytes 8388608 | tf_op jit(solution)/shard_map/all_to_all | solution.py:23
  115.2 5.8 %convolution_convert_fusion.1 = bf16[512,512]{1,0:T(8,128)(2,1)S(1)} fusion(bf16[512,4096]{0,1:T(8,128)(2,1)} %bitcast.99, bf16[4096,512]{1,0:T(8,128)(2,1)} %param.9), kind=kOutput, calls=%fused_computation.15 | convolution fusion | flops 2147745792 | bytes 8912896 | tf_op jit(solution)/shard_map/dot_general | solution.py:27
  121.0 0.9 reshape.113
  121.9 25.4 %collective-permute-done = bf16[2,4,128,128]{3,2,1,0:T(8,128)(2,1)S(1)} collective-permute-done((bf16[2,4,128,128]{3,2,1,0:T(8,128)(2,1)}, bf16[2,4,128,128]{3,2,1,0:T(8,128)(2,1)S(1)}, u32[]{:S(2)}, u32[]{:S(2)}) %collective-permute-start) | collective-permute-done | bytes 262176 | tf_op jit(solution)/shard_map/ppermute | solution.py:15
  147.3 0.7 copy-done.6
  148.0 1.9 collective-permute-start.3
  149.9 1.0 constant_dynamic-update-slice_fusion.8
  150.9 0.0 collective-permute-done.1
  150.9 1.9 collective-permute-start.5
  152.8 1.0 constant_dynamic-update-slice_fusion.7
  153.8 0.0 collective-permute-done.2
  153.8 6.2 %collective-permute-start.4 = (bf16[2,4,128,128]{3,2,1,0:T(8,128)(2,1)}, bf16[2,4,128,128]{3,2,1,0:T(8,128)(2,1)S(1)}, u32[]{:S(2)}, u32[]{:S(2)}) collective-permute-start(bf16[2,4,128,128]{3,2,1,0:T(8,128)(2,1)} %pad_maximum_fusion), channel_id=1, source_target_pairs={{8,0},{16,8},{24,16},{32,24},{40,32},{48,40},{56,48},{64,56},{72,6... | collective-permute-start | bytes 786440 | tf_op jit(solution)/shard_map/ppermute | solution.py:15
  160.1 1.0 constant_dynamic-update-slice_fusion.6
  161.1 0.0 collective-permute-done.3
  161.2 11.4 %collective-permute-done.4 = bf16[2,4,128,128]{3,2,1,0:T(8,128)(2,1)S(1)} collective-permute-done((bf16[2,4,128,128]{3,2,1,0:T(8,128)(2,1)}, bf16[2,4,128,128]{3,2,1,0:T(8,128)(2,1)S(1)}, u32[]{:S(2)}, u32[]{:S(2)}) %collective-permute-start.4) | collective-permute-done | bytes 262176 | tf_op jit(solution)/shard_map/ppermute | solution.py:15
  172.6 0.0 collective-permute-done.5
  172.7 1.0 constant_dynamic-update-slice_fusion.1
  173.6 0.0 collective-permute-done.7
  173.7 3.0 %gather_fusion = bf16[64,2,128,128]{3,2,1,0:T(8,128)(2,1)} fusion(bf16[2,36,128,128]{3,2,1,0:T(8,128)(2,1)S(1)} %constant_dynamic-update-slice_fusion, s32[1024]{0:T(1024)S(1)} %pad_clamp_fusion), kind=kCustom, calls=%fused_computation | custom fusion | bytes 8388864 | tf_op jit(solution)/shard_map/jit(_take)/gather | solution.py:44
  176.7 2.9 %copy.59 = bf16[4,16,2,128,128]{4,3,1,0,2:T(8,128)(2,1)S(1)} copy(bf16[4,16,2,128,128]{4,3,2,1,0:T(8,128)(2,1)} %bitcast.96) | data formatting | bytes 8388608 | tf_op jit(solution)/shard_map/jit(_take)/gather | solution.py:44
  179.7 2.6 %fusion = (f32[4,4,128]{2,1,0:T(4,128)S(1)}, f32[4,16,128,128,4]{3,2,4,1,0:T(8,128)S(1)}) fusion(pred[4,128,16,128]{1,3,2,0:T(8,128)(4,1)S(1)} %copy-done.2, bf16[4,128,4,128,1]{3,2,1,0,4:T(4,128)(2,1)S(1)} %bitcast.100, bf16[2,4,16,128,128]{4,3,2,1,0:T(8,128)(2,1)S(1)} %bitcast.97), kind=kOutput, calls=%fused_computation.4 | convolution fusion | flops 1086322688 | bytes 20455424 | tf_op jit(solution)/shard_map/bqhgd,bskhd->bhgqsk/dot_general | solution.py:65
  182.2 4.3 %fusion.1 = f32[4,4,128]{2,1,0:T(4,128)S(1)} fusion(f32[4,16,128,128,4]{3,2,4,1,0:T(8,128)S(1)} %get-tuple-element.8, f32[4,4,128]{2,1,0:T(4,128)S(1)} %get-tuple-element.7, pred[4,128,16,128]{1,3,2,0:T(8,128)(4,1)S(1)} %copy-done.2), kind=kLoop, calls=%fused_computation.5 | loop fusion | flops 20969472 | bytes 17842176 | tf_op jit(solution)/shard_map/reduce_sum | solution.py:71
  186.6 6.3 %fusion.11 = bf16[4,128,1,4,128]{1,4,3,0,2:T(8,128)(2,1)S(1)} fusion(f32[4,4,128]{2,1,0:T(4,128)S(1)} %fusion.1, f32[4,4,128]{2,1,0:T(4,128)S(1)} %get-tuple-element.7, f32[4,16,128,128,4]{3,2,4,1,0:T(8,128)S(1)} %get-tuple-element.8, pred[4,128,16,128]{1,3,2,0:T(8,128)(4,1)S(1)} %copy-done.2, bf16[2,4,16,128,128]{4,3,2,1,0:T(8,128)(2,1)} %bitcast.98), kind=kOutput, calls=%fused_computation.17 | convolution fusion | flops 1099169792 | bytes 20463616 | tf_op jit(solution)/shard_map/bhgqsk,bskhd->bqhgd/dot_general | solution.py:73
  192.9 0.3 copy.37
  193.2 0.0 copy-start.1
  193.2 6.6 %convolution_convert_fusion = bf16[512,4096]{1,0:T(8,128)(2,1)} fusion(bf16[512,4096]{1,0:T(8,128)(2,1)} %param.12, bf16[64,8,4,128]{3,2,1,0:T(4,128)(2,1)S(1)} %bitcast.101), kind=kOutput, calls=%fused_computation.8 | convolution fusion | flops 2149580800 | bytes 8912896 | tf_op jit(solution)/shard_map/dot_general | solution.py:78
  199.8 0.0 reduce-scatter.2.cloned.1.call-update
  199.8 36.3 %reduce-scatter.2.cloned.1.call-done = bf16[64,4096]{1,0:T(8,128)(2,1)} async-done(((bf16[512,4096]{1,0:T(8,128)(2,1)}), bf16[64,4096]{1,0:T(8,128)(2,1)}) %reduce-scatter.2.cloned.1.call-update) | async-done | bytes 524304 | tf_op jit(solution)/shard_map/reduce_scatter | solution.py:77
  (29 shorter events, 0.2 us)
Async XLA Ops:
  6.5 71.7 %copy-start = (bf16[4096,128]{1,0:T(8,128)(2,1)S(1)}, bf16[4096,128]{1,0:T(8,128)(2,1)}, u32[]{:S(2)}) copy-start(bf16[4096,128]{1,0:T(8,128)(2,1)} %param.11) | copy-start | bytes 3145732
  10.0 4.7 %copy-start.7 = (s32[4,16]{1,0:T(4,128)S(1)}, s32[4,16]{1,0:T(4,128)}, u32[]{:S(2)}) copy-start(s32[4,16]{1,0:T(4,128)} %param.13) | copy-start | bytes 772
  10.0 4.9 %copy-start.9 = (s32[128]{0:T(128)S(1)}, s32[128]{0:T(128)}, u32[]{:S(2)}) copy-start(s32[128]{0:T(128)} %param.15) | copy-start | bytes 1540
  10.0 5.3 %copy-start.8 = (s32[4]{0:T(128)S(1)}, s32[4]{0:T(128)}, u32[]{:S(2)}) copy-start(s32[4]{0:T(128)} %param.14) | copy-start | bytes 52
  10.0 54.3 %all-to-all-start = ((bf16[8,512,512]{2,1,0:T(8,128)(2,1)}), bf16[8,512,512]{2,1,0:T(8,128)(2,1)}, u32[]{:S(2)}, u32[]{:S(2)}) async-start(bf16[8,512,512]{2,1,0:T(8,128)(2,1)} %stack.4), calls=%async_computation | async-start | bytes 8388608 | tf_op jit(solution)/shard_map/all_to_all | solution.py:23
  14.7 221.5 %reduce-scatter.2.cloned.1.call-start = ((), (), s32[]{:S(2)}) async-start(), calls=%async_computation.2 | async-start | bytes 4718592 | tf_op jit(solution)/shard_map/reduce_scatter | solution.py:77
  78.2 3.6 %copy-start.4 = (bf16[4,128,4096]{2,1,0:T(8,128)(2,1)S(1)}, bf16[4,128,4096]{2,1,0:T(8,128)(2,1)}, u32[]{:S(2)}) copy-start(bf16[4,128,4096]{2,1,0:T(8,128)(2,1)} %reshape.109) | copy-start | bytes 12582916
  78.2 3.7 %copy-start.10 = (bf16[4096,128]{1,0:T(8,128)(2,1)S(1)}, bf16[4096,128]{1,0:T(8,128)(2,1)}, u32[]{:S(2)}) copy-start(bf16[4096,128]{1,0:T(8,128)(2,1)} %param.10) | copy-start | bytes 3145732
  84.0 89.7 %collective-permute-start.7 = (bf16[2,4,128,128]{3,2,1,0:T(8,128)(2,1)}, bf16[2,4,128,128]{3,2,1,0:T(8,128)(2,1)S(1)}, u32[]{:S(2)}, u32[]{:S(2)}) collective-permute-start(bf16[2,4,128,128]{3,2,1,0:T(8,128)(2,1)} %pad_maximum_fusion), channel_id=1, source_target_pairs={{32,0},{40,8},{48,16},{56,24},{64,32},{72,40},{80,48},{88,56},{96,... | collective-permute-start | bytes 786440 | tf_op jit(solution)/shard_map/ppermute | solution.py:15
  93.3 79.3 %collective-permute-start.6 = (bf16[2,4,128,128]{3,2,1,0:T(8,128)(2,1)}, bf16[2,4,128,128]{3,2,1,0:T(8,128)(2,1)}, u32[]{:S(2)}, u32[]{:S(2)}) collective-permute-start(bf16[2,4,128,128]{3,2,1,0:T(8,128)(2,1)} %pad_maximum_fusion), channel_id=1, source_target_pairs={{24,0},{32,8},{40,16},{48,24},{56,32},{64,40},{72,48},{80,56},{88,... | collective-permute-start | bytes 786440 | tf_op jit(solution)/shard_map/ppermute | solution.py:15
  95.3 58.6 %collective-permute-start.2 = (bf16[2,4,128,128]{3,2,1,0:T(8,128)(2,1)}, bf16[2,4,128,128]{3,2,1,0:T(8,128)(2,1)}, u32[]{:S(2)}, u32[]{:S(2)}) collective-permute-start(bf16[2,4,128,128]{3,2,1,0:T(8,128)(2,1)} %pad_maximum_fusion), channel_id=1, source_target_pairs={{0,16},{8,24},{16,32},{24,40},{32,48},{40,56},{48,64},{56,72},{64,... | collective-permute-start | bytes 786440 | tf_op jit(solution)/shard_map/ppermute | solution.py:15
  99.6 51.3 %collective-permute-start.1 = (bf16[2,4,128,128]{3,2,1,0:T(8,128)(2,1)}, bf16[2,4,128,128]{3,2,1,0:T(8,128)(2,1)}, u32[]{:S(2)}, u32[]{:S(2)}) collective-permute-start(bf16[2,4,128,128]{3,2,1,0:T(8,128)(2,1)} %pad_maximum_fusion), channel_id=1, source_target_pairs={{0,24},{8,32},{16,40},{24,48},{32,56},{40,64},{48,72},{56,80},{64,... | collective-permute-start | bytes 786440 | tf_op jit(solution)/shard_map/ppermute | solution.py:15
  106.3 41.0 %collective-permute-start = (bf16[2,4,128,128]{3,2,1,0:T(8,128)(2,1)}, bf16[2,4,128,128]{3,2,1,0:T(8,128)(2,1)S(1)}, u32[]{:S(2)}, u32[]{:S(2)}) collective-permute-start(bf16[2,4,128,128]{3,2,1,0:T(8,128)(2,1)} %pad_maximum_fusion), channel_id=1, source_target_pairs={{0,32},{8,40},{16,48},{24,56},{32,64},{40,72},{48,80},{56,88},{64,... | collective-permute-start | bytes 786440 | tf_op jit(solution)/shard_map/ppermute | solution.py:15
  147.3 0.7 copy-start.6
  148.0 13.0 %collective-permute-start.3 = (bf16[2,4,128,128]{3,2,1,0:T(8,128)(2,1)}, bf16[2,4,128,128]{3,2,1,0:T(8,128)(2,1)S(1)}, u32[]{:S(2)}, u32[]{:S(2)}) collective-permute-start(bf16[2,4,128,128]{3,2,1,0:T(8,128)(2,1)} %pad_maximum_fusion), channel_id=1, source_target_pairs={{0,8},{8,16},{16,24},{24,32},{32,40},{40,48},{48,56},{56,64},{64,7... | collective-permute-start | bytes 786440 | tf_op jit(solution)/shard_map/ppermute | solution.py:15
  150.9 21.7 %collective-permute-start.5 = (bf16[2,4,128,128]{3,2,1,0:T(8,128)(2,1)}, bf16[2,4,128,128]{3,2,1,0:T(8,128)(2,1)S(1)}, u32[]{:S(2)}, u32[]{:S(2)}) collective-permute-start(bf16[2,4,128,128]{3,2,1,0:T(8,128)(2,1)} %pad_maximum_fusion), channel_id=1, source_target_pairs={{16,0},{24,8},{32,16},{40,24},{48,32},{56,40},{64,48},{72,56},{80,... | collective-permute-start | bytes 786440 | tf_op jit(solution)/shard_map/ppermute | solution.py:15
  153.8 18.7 %collective-permute-start.4 = (bf16[2,4,128,128]{3,2,1,0:T(8,128)(2,1)}, bf16[2,4,128,128]{3,2,1,0:T(8,128)(2,1)S(1)}, u32[]{:S(2)}, u32[]{:S(2)}) collective-permute-start(bf16[2,4,128,128]{3,2,1,0:T(8,128)(2,1)} %pad_maximum_fusion), channel_id=1, source_target_pairs={{8,0},{16,8},{24,16},{32,24},{40,32},{48,40},{56,48},{64,56},{72,6... | collective-permute-start | bytes 786440 | tf_op jit(solution)/shard_map/ppermute | solution.py:15
  176.7 2.9 %copy-start.2 = (pred[4,128,16,128]{1,3,2,0:T(8,128)(4,1)S(1)}, pred[4,128,16,128]{1,3,2,0:T(8,128)(4,1)}, u32[]{:S(2)}) copy-start(pred[4,128,16,128]{1,3,2,0:T(8,128)(4,1)} %or_and_fusion) | copy-start | bytes 3145732
  176.7 2.9 %copy-start.5 = (bf16[4,128,4,128]{3,2,1,0:T(4,128)(2,1)S(1)}, bf16[4,128,4,128]{3,2,1,0:T(4,128)(2,1)}, u32[]{:S(2)}) copy-start(bf16[4,128,4,128]{3,2,1,0:T(4,128)(2,1)} %reshape.113) | copy-start | bytes 1572868
  179.6 2.6 %copy-start.3 = (bf16[4,16,2,128,128]{4,3,1,0,2:T(8,128)(2,1)}, bf16[4,16,2,128,128]{4,3,1,0,2:T(8,128)(2,1)S(1)}, u32[]{:S(2)}) copy-start(bf16[4,16,2,128,128]{4,3,1,0,2:T(8,128)(2,1)S(1)} %copy.59) | copy-start | bytes 12582916
  193.2 43.0 %copy-start.1 = (bf16[4096,128]{1,0:T(8,128)(2,1)S(1)}, bf16[4096,128]{1,0:T(8,128)(2,1)}, u32[]{:S(2)}) copy-start(bf16[4096,128]{1,0:T(8,128)(2,1)} %param.11) | copy-start | bytes 3145732
Sparse Core Ops, SparseCore 0:
  199.9 36.1 reduce-scatter.1
